TPU v7x, 32 devices: a whole 2x2x4 slice. The times are simulated.
32 devices in a mesh: row: 4 (over z), col: 8 (over y, x, core).
Axes of the slice: x: 2, y: 2, z: 4, core: 2. Of those that a mesh axis runs over, the one named last changes fastest.
Arguments:
- examples: bfloat16 [65536, 1024], P(('row', 'col')), may hold values from -20 to 20
- residuals: float32 [65536, 256], P(('row', 'col')), may hold values from -6 to 6
- coefficients: float32 [65536, 256], P(('row', 'col')), may hold values from -0.8 to 0.8
- block_index: int32 [1], replicated, may hold values from 0 to 63
Outputs:
- new_residuals: float32 [65536, 256], P(('row', 'col'))
- new_coefficients: float32 [65536, 256], P(('row', 'col'))
All inputs are finite; a program needn't handle non-finite values.
Results may differ from a plain program's by a relative error of at most 0.00035.
Values may be sent and summed in bfloat16 or wider, within the bound.
No kernel may reach another device: no remote copies, remote signals or barrier semaphores. Data moves between devices by JAX's collectives and lax.ppermute only.
A program may use at most 128 MiB of HBM per device.

v0:
```python
import jax
import jax.numpy as jnp
from jax import lax
from jax.sharding import PartitionSpec as P

BLOCK = 1024
ridge = 0.001
width_factor = 0.5


def spread(value, axis, source):
    kept = jnp.where(lax.axis_index(axis) == source, value, 0).astype(value.dtype)
    return lax.psum(kept, axis)


def body(examples, residuals, coefficients, block_index):
    rows_here = examples.shape[0]
    features = examples.shape[1]
    per_device = rows_here // BLOCK
    devices_all = lax.axis_size(("row", "col"))
    total_examples = rows_here * devices_all
    chosen = block_index[0]
    owner_rank = chosen // per_device
    offset = chosen % per_device * BLOCK
    my_rank = lax.axis_index(("row", "col"))
    is_owner = owner_rank == my_rank
    my_block = lax.dynamic_slice_in_dim(examples, offset, BLOCK, 0)
    block_rows = spread(my_block, ("row", "col"), owner_rank)
    sq_rows = jnp.sum(jnp.square(examples.astype(jnp.float32)), axis=1)
    sq_block = jnp.sum(jnp.square(block_rows.astype(jnp.float32)), axis=1)
    inner = lax.dot_general(
        examples, block_rows, (((1,), (1,)), ((), ())), preferred_element_type=jnp.float32
    )
    kernel = jnp.exp(
        -width_factor * (sq_rows[:, None] + sq_block[None, :] - 2.0 * inner) / features
    ).astype(jnp.bfloat16)
    residual_low = residuals.astype(jnp.bfloat16)
    grad_part = lax.dot_general(
        kernel, residual_low, (((0,), (0,)), ((), ())), preferred_element_type=jnp.float32
    )
    gram_part = lax.dot_general(
        kernel, kernel, (((0,), (0,)), ((), ())), preferred_element_type=jnp.float32
    )
    own_coef = lax.dynamic_slice_in_dim(coefficients, offset, BLOCK, 0)
    weight_own = jnp.where(is_owner, total_examples * ridge, 0.0).astype(jnp.float32)
    grad_part = grad_part - weight_own * own_coef
    grad, gram_sum = lax.psum((grad_part, gram_part), ("row", "col"))
    system = gram_sum / total_examples + ridge * jnp.eye(BLOCK, dtype=jnp.float32)
    factor = jnp.linalg.cholesky(system)
    update = jax.scipy.linalg.cho_solve((factor, True), grad / total_examples)
    update_low = update.astype(jnp.bfloat16)
    new_residuals = residuals - jnp.dot(kernel, update_low, preferred_element_type=jnp.float32)
    updated = lax.dynamic_update_slice_in_dim(coefficients, own_coef + update, offset, 0)
    new_coefficients = jnp.where(is_owner, updated, coefficients)
    return (new_residuals, new_coefficients)


def solution(mesh):
    in_specs = (P(("row", "col"), None), P(("row", "col"), None), P(("row", "col"), None), P())
    out_specs = (P(("row", "col"), None), P(("row", "col"), None))
    return jax.shard_map(body, mesh=mesh, in_specs=in_specs, out_specs=out_specs, check_vma=False)
```

profile of v0, /device:TPU:0, one launch (start us, length us, event | category | flops | bytes accessed | tf_op | source)
XLA Modules:
  0.0 689.6 jit_solution(11509813493711825370)
XLA Ops:
  7.2 1.6 copy.99
  9.5 3.4 dynamic-slice_select_fusion
  13.0 3.1 multiply_reduce_fusion
  16.1 135.1 %all-reduce.5.cloned.1.call-done = bf16[1024,1024]{1,0:T(8,128)(2,1)} async-done(((bf16[1024,1024]{1,0:T(8,128)(2,1)}), bf16[1024,1024]{1,0:T(8,128)(2,1)}) %all-reduce.5.cloned.1.call-update) | async-done | bytes 2097168 | tf_op jit(solution)/shard_map/psum | solution.py:13
  151.2 2.1 multiply_reduce_fusion.1
  153.3 7.9 %fusion.2 = bf16[2048,1024]{0,1:T(8,128)(2,1)S(1)} fusion(bf16[1024,1024]{1,0:T(8,128)(2,1)} %all-reduce.5.cloned.1.call-done, bf16[2048,1024]{1,0:T(8,128)(2,1)} %param.4, f32[1024]{0:T(1024)S(1)} %multiply_reduce_fusion.1, f32[2048]{0:T(1024)S(1)} %multiply_reduce_fusion), kind=kOutput, calls=%fused_computation.5 | convolution fusion | flops 4305453056 | bytes 10498048 | tf_op jit(solution)/shard_map/dot_general | solution.py:31
  161.2 6.1 fusion.101
  167.2 2.2 convolution_subtract_fusion.1
  169.5 147.1 %all-reduce.7.cloned.1.call-done = (f32[1024,256]{1,0:T(8,128)}, f32[1024,1024]{0,1:T(8,128)}) async-done(((f32[1024,256]{1,0:T(8,128)}, f32[1024,1024]{0,1:T(8,128)}), (f32[1024,256]{1,0:T(8,128)}, f32[1024,1024]{0,1:T(8,128)})) %all-reduce.7.cloned.1.call-update) | async-done | bytes 5242896 | tf_op jit(solution)/shard_map/psum | solution.py:47
  316.6 5.0 select_add_fusion
  321.6 5.5 copy.7
  327.1 4.5 fusion.3
  331.5 2.0 copy-done.1
  333.5 11.7 %cholesky.222 = f32[128,128]{1,0:T(8,128)S(1)} custom-call(f32[128,128]{1,0:T(8,128)S(1)} %cholesky.577), custom_call_target="Cholesky" | custom-call | tf_op jit(solution)/shard_map/jit(cholesky)/cholesky | solution.py:49
  345.4 9.8 %custom-call.66 = f32[1,128,128]{1,2,0:T(8,128)S(1)} custom-call(f32[1,128,128]{2,1,0:T(8,128)S(1)} %get-tuple-element.56), custom_call_target="InvertDiagBlocksLowerTriangular" | custom-call | tf_op jit(solution)/shard_map/jit(cholesky)/cholesky | solution.py:49
  356.9 1.6 convolution_subtract_fusion.2
  359.3 11.7 %cholesky.243 = f32[128,128]{1,0:T(8,128)S(1)} custom-call(f32[128,128]{1,0:T(8,128)S(1)} %cholesky.581), custom_call_target="Cholesky" | custom-call | tf_op jit(solution)/shard_map/jit(cholesky)/cholesky | solution.py:49
  371.3 2.5 cholesky.254
  373.8 9.8 %custom-call.67 = f32[1,128,128]{1,2,0:T(8,128)S(1)} custom-call(f32[1,128,128]{2,1,0:T(8,128)S(1)} %get-tuple-element.54), custom_call_target="InvertDiagBlocksLowerTriangular" | custom-call | tf_op jit(solution)/shard_map/jit(cholesky)/cholesky | solution.py:49
  386.5 2.7 convolution_subtract_fusion.3
  389.2 11.7 %cholesky.466 = f32[128,128]{1,0:T(8,128)S(1)} custom-call(f32[128,128]{1,0:T(8,128)S(1)} %cholesky.586), custom_call_target="Cholesky" | custom-call | tf_op jit(solution)/shard_map/jit(cholesky)/cholesky | solution.py:49
  401.7 9.8 %custom-call.68 = f32[1,128,128]{1,2,0:T(8,128)S(1)} custom-call(f32[1,128,128]{2,1,0:T(8,128)S(1)} %get-tuple-element.52), custom_call_target="InvertDiagBlocksLowerTriangular" | custom-call | tf_op jit(solution)/shard_map/jit(cholesky)/cholesky | solution.py:49
  412.7 3.5 convolution_subtract_fusion.4
  416.3 11.7 %cholesky.485 = f32[128,128]{1,0:T(8,128)S(1)} custom-call(f32[128,128]{1,0:T(8,128)S(1)} %cholesky.591), custom_call_target="Cholesky" | custom-call | tf_op jit(solution)/shard_map/jit(cholesky)/cholesky | solution.py:49
  428.7 9.8 %custom-call.69 = f32[1,128,128]{1,2,0:T(8,128)S(1)} custom-call(f32[1,128,128]{2,1,0:T(8,128)S(1)} %get-tuple-element.50), custom_call_target="InvertDiagBlocksLowerTriangular" | custom-call | tf_op jit(solution)/shard_map/jit(cholesky)/cholesky | solution.py:49
  439.7 3.2 convolution_subtract_fusion.5
  442.9 11.9 %cholesky.504 = f32[128,128]{1,0:T(8,128)S(1)} custom-call(f32[128,128]{1,0:T(8,128)S(1)} %cholesky.596), custom_call_target="Cholesky" | custom-call | tf_op jit(solution)/shard_map/jit(cholesky)/cholesky | solution.py:49
  455.5 9.8 %custom-call.70 = f32[1,128,128]{1,2,0:T(8,128)S(1)} custom-call(f32[1,128,128]{2,1,0:T(8,128)S(1)} %get-tuple-element.48), custom_call_target="InvertDiagBlocksLowerTriangular" | custom-call | tf_op jit(solution)/shard_map/jit(cholesky)/cholesky | solution.py:49
  466.5 3.2 convolution_subtract_fusion.6
  469.7 11.7 %cholesky.524 = f32[128,128]{1,0:T(8,128)S(1)} custom-call(f32[128,128]{1,0:T(8,128)S(1)} %cholesky.601), custom_call_target="Cholesky" | custom-call | tf_op jit(solution)/shard_map/jit(cholesky)/cholesky | solution.py:49
  482.2 9.8 %custom-call.71 = f32[1,128,128]{1,2,0:T(8,128)S(1)} custom-call(f32[1,128,128]{2,1,0:T(8,128)S(1)} %get-tuple-element.46), custom_call_target="InvertDiagBlocksLowerTriangular" | custom-call | tf_op jit(solution)/shard_map/jit(cholesky)/cholesky | solution.py:49
  493.0 3.1 convolution_subtract_fusion.19
  496.2 11.7 %cholesky.544 = f32[128,128]{1,0:T(8,128)S(1)} custom-call(f32[128,128]{1,0:T(8,128)S(1)} %cholesky.606), custom_call_target="Cholesky" | custom-call | tf_op jit(solution)/shard_map/jit(cholesky)/cholesky | solution.py:49
  508.6 9.8 %custom-call.72 = f32[1,128,128]{1,2,0:T(8,128)S(1)} custom-call(f32[1,128,128]{2,1,0:T(8,128)S(1)} %get-tuple-element.44), custom_call_target="InvertDiagBlocksLowerTriangular" | custom-call | tf_op jit(solution)/shard_map/jit(cholesky)/cholesky | solution.py:49
  519.4 2.2 convolution_subtract_fusion.22
  521.6 11.7 %cholesky.562 = f32[128,128]{1,0:T(8,128)S(1)} custom-call(f32[128,128]{1,0:T(8,128)S(1)} %convolution_subtract_fusion.22), custom_call_target="Cholesky" | custom-call | tf_op jit(solution)/shard_map/jit(cholesky)/cholesky | solution.py:49
  545.0 4.9 select_select_fusion
  549.9 28.3 %while.1 = (s32[]{:T(128)}, f32[1024,1024]{0,1:T(8,128)}, s32[8,2]{0,1:T(2,128)S(1)}, f32[8,128,128]{2,1,0:T(8,128)}, s32[]{:T(128)}) while((s32[]{:T(128)}, f32[1024,1024]{0,1:T(8,128)}, s32[8,2]{0,1:T(2,128)S(1)}, f32[8,128,128]{2,1,0:T(8,128)}, s32[]{:T(128)}) %tuple.53), condition=%wide.while_cond, body=%wide.while_body.sunk | while | flops 2 | bytes 393329 | solution.py:50
  550.5 2.2 dynamic-slice.9
  554.0 2.2 dynamic-slice.9
  557.6 2.2 dynamic-slice.9
  561.1 2.2 dynamic-slice.9
  564.7 2.2 dynamic-slice.9
  568.2 2.2 dynamic-slice.9
  571.8 2.2 dynamic-slice.9
  575.3 2.1 dynamic-slice.9
  578.2 80.2 %custom-call.73 = f32[8,128,128]{1,2,0:T(8,128)} custom-call(f32[8,128,128]{2,1,0:T(8,128)} %get-tuple-element.9), custom_call_target="InvertDiagBlocksLowerTriangular" | custom-call | tf_op jit(solution)/shard_map/jit(_cho_solve)/triangular_solve | solution.py:50
  678.2 2.8 convolution_subtract_fusion
  (158 shorter events, 53.5 us)
Async XLA Ops:
  7.2 144.0 %all-reduce.5.cloned.1.call-start = ((), (), s32[]{:S(2)}) async-start(), calls=%async_computation | async-start | bytes 4194304 | tf_op jit(solution)/shard_map/psum | solution.py:13
  13.0 303.6 %all-reduce.7.cloned.1.call-start = ((), (), s32[]{:S(2)}) async-start(), calls=%async_computation.1 | async-start | bytes 10485760 | tf_op jit(solution)/shard_map/psum | solution.py:47
  161.1 6.1 copy-start.2
  161.1 6.1 copy-start.5
  331.5 2.0 copy-start.1
  358.5 0.8 copy-start.8
  359.3 25.9 %copy-start.9 = (f32[896,128]{1,0:T(8,128)S(1)}, f32[896,128]{1,0:T(8,128)}, u32[]{:S(2)}) copy-start(f32[896,128]{1,0:T(8,128)} %copy-done.8) | copy-start | bytes 1376260
  658.4 8.8 %copy-start = (f32[1024,1024]{0,1:T(8,128)S(1)}, f32[1024,1024]{0,1:T(8,128)}, u32[]{:S(2)}) copy-start(f32[1024,1024]{0,1:T(8,128)} %get-tuple-element.124) | copy-start | bytes 12582916
  658.4 9.5 %copy-start.7 = (f32[8,128,128]{1,2,0:T(8,128)S(1)}, f32[8,128,128]{1,2,0:T(8,128)}, u32[]{:S(2)}) copy-start(f32[8,128,128]{1,2,0:T(8,128)} %custom-call.73) | copy-start | bytes 1572868
  675.4 2.2 copy-start.3
  675.4 2.9 copy-start.6
  681.2 1.3 copy-start.4
Sparse Core Ops, SparseCore 0:
  13.9 137.2 all-reduce.4
  169.6 146.9 all-reduce.6
where the time goes:
time: 698 us; the launch traced here: 690 us
  waiting for transfers between devices  282 us (40%)
  other arithmetic  272 us (39%)
  matrix products  65 us (9%)
  local copies, waits for them, and re-layouts  49.5 us (7%)
  between operations  20.7 us (3%)
    another operation x30, other arithmetic, body(): factor = jnp.linalg.cholesky(system)  167 us
    psum x1, waiting for transfers between devices, body(): grad, gram_sum = lax.psum((grad_part, gram_part), ('row', 'col'))  147 us
    psum x1, waiting for transfers between devices, spread(): return lax.psum(kept, axis)  135 us
    another operation x3, other arithmetic, body(): update = jax.scipy.linalg.cho_solve((factor, True), grad / total_examples)  85.1 us
    another operation x40, local copies, waits for them, and re-layouts  28.2 us
    another operation x14, matrix products, body(): factor = jnp.linalg.cholesky(system)  27.7 us
    another operation x30, matrix products, body(): update = jax.scipy.linalg.cho_solve((factor, True), grad / total_examples)  18.3 us
  transfers between devices with their start and end apart: 2, of which 2 were waited for; matrix products, arithmetic and copies ran while one was open for 0% of the time, Pallas kernels for 0%

commit v1 on v0

--- a/solution.py
+++ b/solution.py
@@ -44,7 +44,7 @@
     own_coef = lax.dynamic_slice_in_dim(coefficients, offset, BLOCK, 0)
     weight_own = jnp.where(is_owner, total_examples * ridge, 0.0).astype(jnp.float32)
     grad_part = grad_part - weight_own * own_coef
-    grad, gram_sum = lax.psum((grad_part, gram_part), ("row", "col"))
+    grad, gram_sum = lax.psum(lax.psum((grad_part, gram_part), "col"), "row")
     system = gram_sum / total_examples + ridge * jnp.eye(BLOCK, dtype=jnp.float32)
     factor = jnp.linalg.cholesky(system)
     update = jax.scipy.linalg.cho_solve((factor, True), grad / total_examples)

time: 698 us -> 834 us (1.19)
  waiting for transfers between devices: 282 us -> 418 us
    psum x1 -> x2, waiting for transfers between devices: 147 us -> 283 us  [body(): grad, gram_sum = lax.psum(lax.psum((grad_part, gram_part), 'col'), 'row')]
  transfers between devices with their start and end apart: 2 -> 3, of which waited for: 2 -> 3; matrix products, arithmetic and copies ran while one was open for 0% -> 0% of each run, Pallas kernels for 0% -> 0%
where the time goes in v1:
time: 834 us; the launch traced here: 825 us
  waiting for transfers between devices  418 us (50%)
  other arithmetic  272 us (33%)
  matrix products  65 us (8%)
  local copies, waits for them, and re-layouts  49.5 us (6%)
  between operations  20.4 us (2%)
    psum x2, waiting for transfers between devices, body(): grad, gram_sum = lax.psum(lax.psum((grad_part, gram_part), 'col'), 'row')  283 us
    another operation x30, other arithmetic, body(): factor = jnp.linalg.cholesky(system)  167 us
    psum x1, waiting for transfers between devices, spread(): return lax.psum(kept, axis)  135 us
    another operation x3, other arithmetic, body(): update = jax.scipy.linalg.cho_solve((factor, True), grad / total_examples)  85.1 us
    another operation x40, local copies, waits for them, and re-layouts  28.2 us
    another operation x14, matrix products, body(): factor = jnp.linalg.cholesky(system)  27.7 us
    another operation x30, matrix products, body(): update = jax.scipy.linalg.cho_solve((factor, True), grad / total_examples)  18.3 us
  transfers between devices with their start and end apart: 3, of which 3 were waited for; matrix products, arithmetic and copies ran while one was open for 0% of the time, Pallas kernels for 0%

profile of v1, /device:TPU:0, one launch (start us, length us, event | category | flops | bytes accessed | tf_op | source)
XLA Modules:
  0.0 825.0 jit_solution(1578960839506162668)
XLA Ops:
  7.2 1.6 copy.101
  9.5 3.4 dynamic-slice_select_fusion
  13.0 3.1 multiply_reduce_fusion
  16.1 135.1 %all-reduce.7.cloned.1.call-done = bf16[1024,1024]{1,0:T(8,128)(2,1)} async-done(((bf16[1024,1024]{1,0:T(8,128)(2,1)}), bf16[1024,1024]{1,0:T(8,128)(2,1)}) %all-reduce.7.cloned.1.call-update) | async-done | bytes 2097168 | tf_op jit(solution)/shard_map/psum | solution.py:13
  151.2 2.1 multiply_reduce_fusion.1
  153.3 7.9 fusion.2
  161.2 6.1 fusion.101
  167.3 2.2 convolution_subtract_fusion.1
  169.6 91.2 %all-reduce.9.cloned.1.call-done = (f32[1024,256]{1,0:T(8,128)}, f32[1024,1024]{0,1:T(8,128)}) async-done(((f32[1024,256]{1,0:T(8,128)}, f32[1024,1024]{0,1:T(8,128)}), (f32[1024,256]{1,0:T(8,128)}, f32[1024,1024]{0,1:T(8,128)})) %all-reduce.9.cloned.1.call-update) | async-done | bytes 5242896 | tf_op jit(solution)/shard_map/psum | solution.py:47
  260.9 191.5 %all-reduce.11.cloned.1.call-done = (f32[1024,256]{1,0:T(8,128)}, f32[1024,1024]{0,1:T(8,128)}) async-done(((f32[1024,256]{1,0:T(8,128)}, f32[1024,1024]{0,1:T(8,128)}), (f32[1024,256]{1,0:T(8,128)}, f32[1024,1024]{0,1:T(8,128)})) %all-reduce.11.cloned.1.call-update) | async-done | bytes 5242896 | tf_op jit(solution)/shard_map/psum | solution.py:47
  452.4 5.0 select_add_fusion
  457.4 5.5 copy.7
  462.9 4.5 fusion.3
  467.3 2.0 copy-done.1
  469.3 11.7 %cholesky.222 = f32[128,128]{1,0:T(8,128)S(1)} custom-call(f32[128,128]{1,0:T(8,128)S(1)} %cholesky.577), custom_call_target="Cholesky" | custom-call | tf_op jit(solution)/shard_map/jit(cholesky)/cholesky | solution.py:49
  481.2 9.8 %custom-call.66 = f32[1,128,128]{1,2,0:T(8,128)S(1)} custom-call(f32[1,128,128]{2,1,0:T(8,128)S(1)} %get-tuple-element.58), custom_call_target="InvertDiagBlocksLowerTriangular" | custom-call | tf_op jit(solution)/shard_map/jit(cholesky)/cholesky | solution.py:49
  495.0 11.7 %cholesky.243 = f32[128,128]{1,0:T(8,128)S(1)} custom-call(f32[128,128]{1,0:T(8,128)S(1)} %cholesky.581), custom_call_target="Cholesky" | custom-call | tf_op jit(solution)/shard_map/jit(cholesky)/cholesky | solution.py:49
  507.1 2.5 cholesky.254
  509.6 9.8 %custom-call.67 = f32[1,128,128]{1,2,0:T(8,128)S(1)} custom-call(f32[1,128,128]{2,1,0:T(8,128)S(1)} %get-tuple-element.56), custom_call_target="InvertDiagBlocksLowerTriangular" | custom-call | tf_op jit(solution)/shard_map/jit(cholesky)/cholesky | solution.py:49
  522.3 2.7 convolution_subtract_fusion.3
  525.0 11.7 %cholesky.466 = f32[128,128]{1,0:T(8,128)S(1)} custom-call(f32[128,128]{1,0:T(8,128)S(1)} %cholesky.586), custom_call_target="Cholesky" | custom-call | tf_op jit(solution)/shard_map/jit(cholesky)/cholesky | solution.py:49
  537.5 9.8 %custom-call.68 = f32[1,128,128]{1,2,0:T(8,128)S(1)} custom-call(f32[1,128,128]{2,1,0:T(8,128)S(1)} %get-tuple-element.54), custom_call_target="InvertDiagBlocksLowerTriangular" | custom-call | tf_op jit(solution)/shard_map/jit(cholesky)/cholesky | solution.py:49
  548.5 3.5 convolution_subtract_fusion.4
  552.0 11.7 %cholesky.485 = f32[128,128]{1,0:T(8,128)S(1)} custom-call(f32[128,128]{1,0:T(8,128)S(1)} %cholesky.591), custom_call_target="Cholesky" | custom-call | tf_op jit(solution)/shard_map/jit(cholesky)/cholesky | solution.py:49
  564.5 9.8 %custom-call.69 = f32[1,128,128]{1,2,0:T(8,128)S(1)} custom-call(f32[1,128,128]{2,1,0:T(8,128)S(1)} %get-tuple-element.52), custom_call_target="InvertDiagBlocksLowerTriangular" | custom-call | tf_op jit(solution)/shard_map/jit(cholesky)/cholesky | solution.py:49
  575.5 3.2 convolution_subtract_fusion.5
  578.6 11.9 %cholesky.504 = f32[128,128]{1,0:T(8,128)S(1)} custom-call(f32[128,128]{1,0:T(8,128)S(1)} %cholesky.596), custom_call_target="Cholesky" | custom-call | tf_op jit(solution)/shard_map/jit(cholesky)/cholesky | solution.py:49
  591.3 9.8 %custom-call.70 = f32[1,128,128]{1,2,0:T(8,128)S(1)} custom-call(f32[1,128,128]{2,1,0:T(8,128)S(1)} %get-tuple-element.50), custom_call_target="InvertDiagBlocksLowerTriangular" | custom-call | tf_op jit(solution)/shard_map/jit(cholesky)/cholesky | solution.py:49
  602.2 3.2 convolution_subtract_fusion.6
  605.5 11.7 %cholesky.524 = f32[128,128]{1,0:T(8,128)S(1)} custom-call(f32[128,128]{1,0:T(8,128)S(1)} %cholesky.601), custom_call_target="Cholesky" | custom-call | tf_op jit(solution)/shard_map/jit(cholesky)/cholesky | solution.py:49
  618.0 9.8 %custom-call.71 = f32[1,128,128]{1,2,0:T(8,128)S(1)} custom-call(f32[1,128,128]{2,1,0:T(8,128)S(1)} %get-tuple-element.48), custom_call_target="InvertDiagBlocksLowerTriangular" | custom-call | tf_op jit(solution)/shard_map/jit(cholesky)/cholesky | solution.py:49
  628.8 3.1 convolution_subtract_fusion.19
  631.9 11.7 %cholesky.544 = f32[128,128]{1,0:T(8,128)S(1)} custom-call(f32[128,128]{1,0:T(8,128)S(1)} %cholesky.606), custom_call_target="Cholesky" | custom-call | tf_op jit(solution)/shard_map/jit(cholesky)/cholesky | solution.py:49
  644.4 9.8 %custom-call.72 = f32[1,128,128]{1,2,0:T(8,128)S(1)} custom-call(f32[1,128,128]{2,1,0:T(8,128)S(1)} %get-tuple-element.46), custom_call_target="InvertDiagBlocksLowerTriangular" | custom-call | tf_op jit(solution)/shard_map/jit(cholesky)/cholesky | solution.py:49
  655.2 2.2 convolution_subtract_fusion.22
  657.4 11.7 %cholesky.562 = f32[128,128]{1,0:T(8,128)S(1)} custom-call(f32[128,128]{1,0:T(8,128)S(1)} %convolution_subtract_fusion.22), custom_call_target="Cholesky" | custom-call | tf_op jit(solution)/shard_map/jit(cholesky)/cholesky | solution.py:49
  680.8 4.9 select_select_fusion
  685.6 28.3 %while.1 = (s32[]{:T(128)}, f32[1024,1024]{0,1:T(8,128)}, s32[8,2]{0,1:T(2,128)S(1)}, f32[8,128,128]{2,1,0:T(8,128)}, s32[]{:T(128)}) while((s32[]{:T(128)}, f32[1024,1024]{0,1:T(8,128)}, s32[8,2]{0,1:T(2,128)S(1)}, f32[8,128,128]{2,1,0:T(8,128)}, s32[]{:T(128)}) %tuple.53), condition=%wide.while_cond, body=%wide.while_body.sunk | while | flops 2 | bytes 393329 | solution.py:50
  686.2 2.2 dynamic-slice.9
  689.8 2.2 dynamic-slice.9
  693.3 2.2 dynamic-slice.9
  696.9 2.2 dynamic-slice.9
  700.4 2.2 dynamic-slice.9
  704.0 2.2 dynamic-slice.9
  707.5 2.2 dynamic-slice.9
  711.1 2.1 dynamic-slice.9
  714.0 80.2 %custom-call.73 = f32[8,128,128]{1,2,0:T(8,128)} custom-call(f32[8,128,128]{2,1,0:T(8,128)} %get-tuple-element.9), custom_call_target="InvertDiagBlocksLowerTriangular" | custom-call | tf_op jit(solution)/shard_map/jit(_cho_solve)/triangular_solve | solution.py:50
  814.0 2.8 convolution_subtract_fusion
  (161 shorter events, 55.1 us)
Async XLA Ops:
  7.2 144.0 %all-reduce.7.cloned.1.call-start = ((), (), s32[]{:S(2)}) async-start(), calls=%async_computation | async-start | bytes 4194304 | tf_op jit(solution)/shard_map/psum | solution.py:13
  13.0 247.9 %all-reduce.9.cloned.1.call-start = ((), (), s32[]{:S(2)}) async-start(), calls=%async_computation.1 | async-start | bytes 10485760 | tf_op jit(solution)/shard_map/psum | solution.py:47
  161.1 6.1 copy-start.2
  161.1 6.1 copy-start.5
  169.5 282.8 %all-reduce.11.cloned.1.call-start = ((), (), s32[]{:S(2)}) async-start(), calls=%async_computation.2 | async-start | bytes 10485760 | tf_op jit(solution)/shard_map/psum | solution.py:47
  467.3 2.0 copy-start.1
  494.3 0.8 copy-start.8
  495.0 25.9 %copy-start.9 = (f32[896,128]{1,0:T(8,128)S(1)}, f32[896,128]{1,0:T(8,128)}, u32[]{:S(2)}) copy-start(f32[896,128]{1,0:T(8,128)} %copy-done.8) | copy-start | bytes 1376260
  794.2 8.8 %copy-start = (f32[1024,1024]{0,1:T(8,128)S(1)}, f32[1024,1024]{0,1:T(8,128)}, u32[]{:S(2)}) copy-start(f32[1024,1024]{0,1:T(8,128)} %get-tuple-element.130) | copy-start | bytes 12582916
  794.2 9.5 %copy-start.7 = (f32[8,128,128]{1,2,0:T(8,128)S(1)}, f32[8,128,128]{1,2,0:T(8,128)}, u32[]{:S(2)}) copy-start(f32[8,128,128]{1,2,0:T(8,128)} %custom-call.73) | copy-start | bytes 1572868
  811.1 2.2 copy-start.3
  811.1 2.9 copy-start.6
  817.0 1.3 copy-start.4
Sparse Core Ops, SparseCore 0:
  13.9 137.2 all-reduce.6
  169.7 91.1 all-reduce.8
  263.3 189.0 all-reduce.10
